TPU v7x, 32 devices: a whole 2x2x4 slice. The times are simulated.
32 devices in a mesh: fsdp: 4 (over z), ctx: 4 (over y, x), tp: 2 (over core).
Axes of the slice: x: 2, y: 2, z: 4, core: 2. Of those that a mesh axis runs over, the one named last changes fastest.
Arguments:
- hidden_in: bfloat16 [16, 1024, 768], P('fsdp', 'ctx'), may hold values from -6 to 6
- lengths: int32 [16], P('fsdp'), may hold values from 256 to 1024, as said below
- out_grad: bfloat16 [16, 1024, 768], P('fsdp', 'ctx'), may hold values from -6 to 6
- w_qkv: bfloat16 [3, 768, 768], P(None, 'fsdp', 'tp'), may hold values from -0.21875 to 0.21875
- qv_bias: bfloat16 [2, 12, 64], P(None, 'tp', 'fsdp'), may hold values from -0.3125 to 0.3125
- w_out: bfloat16 [768, 768], P('tp', 'fsdp'), may hold values from -3.5 to 3.5
- out_biases: bfloat16 [2, 768], P(None, 'fsdp'), may hold values from -4 to 4
- norm_gains: bfloat16 [2, 768], P(None, 'fsdp'), may hold values from 0.25 to 1.75
- norm_biases: bfloat16 [2, 768], P(None, 'fsdp'), may hold values from -4 to 4
- w_in: bfloat16 [768, 3072], P(None, ('fsdp', 'tp')), may hold values from -0.21875 to 0.21875
- ffn_bias: bfloat16 [3072], P(('fsdp', 'tp')), may hold values from -6 to 6
- w_ffo: bfloat16 [3072, 768], P(('fsdp', 'tp')), may hold values from -0.109375 to 0.109375
Outputs:
- hidden_out: bfloat16 [16, 1024, 768], P('fsdp', 'ctx')
- hidden_grad: bfloat16 [16, 1024, 768], P('fsdp', 'ctx')
- grad_qkv: float32 [3, 768, 768], P(None, 'fsdp', 'tp')
- grad_qv_bias: float32 [2, 12, 64], P(None, 'tp', 'fsdp')
- grad_out: float32 [768, 768], P('tp', 'fsdp')
- grad_out_biases: float32 [2, 768], P(None, 'fsdp')
- grad_gains: float32 [2, 768], P(None, 'fsdp')
- grad_shifts: float32 [2, 768], P(None, 'fsdp')
- grad_in: float32 [768, 3072], P(None, ('fsdp', 'tp'))
- grad_ffn_bias: float32 [3072], P(('fsdp', 'tp'))
- grad_ffo: float32 [3072, 768], P(('fsdp', 'tp'))
Inputs may be any that keep to these rules, and one draw needn't show every extreme that they name: lengths[s] counts the valid positions of slot s from its start; in every draw one slot has 1024 and one has 256.
All inputs are finite; a program needn't handle non-finite values.
Results may differ from a plain program's by a relative error of at most 0.019.
Values may be sent and summed in bfloat16 or wider, within the bound.
A program may use at most 192 MiB of HBM per device.

v0:
```python
import jax
import jax.numpy as jnp
from jax import lax
from jax.sharding import PartitionSpec as P

epsilon = 1e-05
masked_value = -1e30
heads_together = 2


def norm_rows(residual, gain_row, shift_row):
    centre = jnp.mean(residual, axis=-1, keepdims=True)
    centred = residual - centre
    spread = jnp.mean(centred * centred, axis=-1, keepdims=True)
    return centred * lax.rsqrt(spread + epsilon) * gain_row + shift_row


def gelu_exact(values):
    return jax.nn.gelu(values, approximate=False)


def split_heads(matrix, head_dim):
    return matrix.reshape(matrix.shape[0], matrix.shape[1] // head_dim, head_dim)


def block_scores(query_heads, key_heads, key_mask, score_scale):
    scores = (
        jnp.einsum("qhd,khd->hqk", query_heads, key_heads, preferred_element_type=jnp.float32)
        * score_scale
    )
    return jnp.where(key_mask[None, None, :], scores, masked_value)


def attend_slot(queries, key_value, length, score_scale, head_dim):
    gathered = lax.all_gather(key_value, "ctx", axis=1, tiled=True)
    seq_len = gathered.shape[1]
    key_mask = lax.iota(jnp.int32, seq_len) < length
    block_width = heads_together * head_dim
    outputs = []
    totals = []
    for head_block in range(queries.shape[1] // block_width):
        columns = slice(head_block * block_width, (head_block + 1) * block_width)
        query_heads = split_heads(queries[:, columns], head_dim)
        key_heads = split_heads(gathered[0][:, columns], head_dim)
        value_heads = split_heads(gathered[1][:, columns], head_dim)
        scores = block_scores(query_heads, key_heads, key_mask, score_scale)
        highest = jnp.max(scores, axis=-1, keepdims=True)
        log_total = highest + jnp.log(jnp.sum(jnp.exp(scores - highest), axis=-1, keepdims=True))
        weights_low = jnp.exp(scores - log_total).astype(jnp.bfloat16)
        attended = jnp.einsum(
            "hqk,khd->qhd", weights_low, value_heads, preferred_element_type=jnp.float32
        )
        outputs.append(attended.reshape(attended.shape[0], block_width))
        totals.append(log_total[:, :, 0])
    return (jnp.concatenate(outputs, axis=1).astype(jnp.bfloat16), jnp.concatenate(totals, axis=0))


def slot_grads(queries, key_value, length, grad_mixed, log_totals, score_scale, head_dim):
    gathered = lax.all_gather(key_value, "ctx", axis=1, tiled=True)
    seq_len = gathered.shape[1]
    key_mask = lax.iota(jnp.int32, seq_len) < length
    block_width = heads_together * head_dim
    query_grads = []
    key_grads = []
    value_grads = []
    inner_parts = []
    for head_block in range(queries.shape[1] // block_width):
        columns = slice(head_block * block_width, (head_block + 1) * block_width)
        heads_range = slice(head_block * heads_together, (head_block + 1) * heads_together)
        query_heads = split_heads(queries[:, columns], head_dim)
        key_heads = split_heads(gathered[0][:, columns], head_dim)
        value_heads = split_heads(gathered[1][:, columns], head_dim)
        grad_heads = split_heads(grad_mixed[:, columns], head_dim)
        scores = block_scores(query_heads, key_heads, key_mask, score_scale)
        softmax_rows = jnp.exp(scores - log_totals[heads_range, :, None])
        grad_weights = jnp.einsum(
            "qhd,khd->hqk", grad_heads, value_heads, preferred_element_type=jnp.float32
        )
        inner_sums = jnp.sum(softmax_rows * grad_weights, axis=-1)
        grad_scores = (softmax_rows * (grad_weights - inner_sums[:, :, None])).astype(jnp.bfloat16)
        grad_query = (
            jnp.einsum("hqk,khd->qhd", grad_scores, key_heads, preferred_element_type=jnp.float32)
            * score_scale
        )
        query_grads.append(grad_query.reshape(grad_query.shape[0], block_width))
        inner_parts.append(inner_sums)
        grad_key = (
            jnp.einsum("hqk,qhd->khd", grad_scores, query_heads, preferred_element_type=jnp.float32)
            * score_scale
        )
        grad_value = jnp.einsum(
            "hqk,qhd->khd",
            softmax_rows.astype(jnp.bfloat16),
            grad_heads,
            preferred_element_type=jnp.float32,
        )
        key_grads.append(grad_key.reshape(seq_len, block_width))
        value_grads.append(grad_value.reshape(seq_len, block_width))
    grad_queries = jnp.concatenate(query_grads, axis=1)
    key_terms = jnp.stack(
        [jnp.concatenate(key_grads, axis=1), jnp.concatenate(value_grads, axis=1)]
    )
    own_grads = lax.psum_scatter(
        key_terms.astype(jnp.bfloat16), "ctx", scatter_dimension=1, tiled=True
    ).astype(jnp.float32)
    return (grad_queries, own_grads)


def per_device(
    hidden_in,
    lengths,
    out_grad,
    w_qkv,
    qv_bias,
    w_out,
    out_biases,
    norm_gains,
    norm_biases,
    w_in,
    ffn_bias,
    w_ffo,
):
    w_proj, proj_bias, w_back, branch_biases, gains, shifts, w_up, up_bias, w_down = (
        lax.all_gather(w_qkv, "fsdp", axis=1, tiled=True),
        lax.all_gather(qv_bias, "fsdp", axis=2, tiled=True),
        lax.all_gather(w_out, "fsdp", axis=1, tiled=True),
        lax.all_gather(out_biases, "fsdp", axis=1, tiled=True),
        lax.all_gather(norm_gains, "fsdp", axis=1, tiled=True),
        lax.all_gather(norm_biases, "fsdp", axis=1, tiled=True),
        lax.all_gather(w_in, "fsdp", axis=1, tiled=True),
        lax.all_gather(ffn_bias, "fsdp", axis=0, tiled=True),
        lax.all_gather(w_ffo, "fsdp", axis=0, tiled=True),
    )
    slot_count, block_len, model_width = hidden_in.shape
    token_count = slot_count * block_len
    head_dim = proj_bias.shape[2]
    score_scale = head_dim ** (-0.5)
    local_width = w_proj.shape[2]
    contract_rows = (((0,), (0,)), ((), ()))
    contract_cols = (((1,), (1,)), ((), ()))
    bias_table = jnp.stack(
        [
            proj_bias[0].reshape(local_width).astype(jnp.float32),
            jnp.zeros((local_width,), jnp.float32),
            proj_bias[1].reshape(local_width).astype(jnp.float32),
        ]
    )
    projected = (
        jnp.einsum("sbd,pdc->spbc", hidden_in, w_proj, preferred_element_type=jnp.float32)
        + bias_table[None, :, None, :]
    ).astype(jnp.bfloat16)
    queries = projected[:, 0]
    key_values = projected[:, 1:]
    attended, log_totals = lax.map(
        lambda slot_items: attend_slot(
            slot_items[0], slot_items[1], slot_items[2], score_scale, head_dim
        ),
        (queries, key_values, lengths),
    )
    mixed_rows = attended.reshape(token_count, local_width)
    token_rows = hidden_in.reshape(token_count, model_width)
    branch = lax.psum(
        jnp.dot(mixed_rows, w_back, preferred_element_type=jnp.float32), "tp"
    ) + branch_biases[0].astype(jnp.float32)
    first_norm, first_pull = jax.vjp(
        norm_rows,
        token_rows.astype(jnp.float32) + branch,
        gains[0].astype(jnp.float32),
        shifts[0].astype(jnp.float32),
    )
    first_low = first_norm.astype(jnp.bfloat16)
    hidden_pre = jnp.dot(first_low, w_up, preferred_element_type=jnp.float32) + up_bias.astype(
        jnp.float32
    )
    activated, gelu_pull = jax.vjp(gelu_exact, hidden_pre)
    activated_low = activated.astype(jnp.bfloat16)
    second_branch = lax.psum(
        jnp.dot(activated_low, w_down, preferred_element_type=jnp.float32), "tp"
    ) + branch_biases[1].astype(jnp.float32)
    output_rows, second_pull = jax.vjp(
        norm_rows,
        first_norm + second_branch,
        gains[1].astype(jnp.float32),
        shifts[1].astype(jnp.float32),
    )
    hidden_out = output_rows.astype(jnp.bfloat16).reshape(slot_count, block_len, model_width)
    own_start = lax.axis_index("ctx") * block_len
    positions = own_start + lax.iota(jnp.int32, block_len)
    row_mask = (positions[None, :] < lengths[:, None]).astype(jnp.float32).reshape(token_count, 1)
    grad_output = out_grad.reshape(token_count, model_width).astype(jnp.float32) * row_mask
    grad_second, grad_gain_two, grad_shift_two = second_pull(grad_output)
    grad_second_low = grad_second.astype(jnp.bfloat16)
    grad_down = lax.dot_general(
        activated_low, grad_second_low, contract_rows, preferred_element_type=jnp.float32
    )
    grad_act = lax.dot_general(
        grad_second_low, w_down, contract_cols, preferred_element_type=jnp.float32
    )
    (grad_pre,) = gelu_pull(grad_act)
    grad_pre_low = grad_pre.astype(jnp.bfloat16)
    grad_up = lax.dot_general(
        first_low, grad_pre_low, contract_rows, preferred_element_type=jnp.float32
    )
    grad_first = grad_second + lax.psum(
        lax.dot_general(grad_pre_low, w_up, contract_cols, preferred_element_type=jnp.float32), "tp"
    )
    grad_resid, grad_gain_one, grad_shift_one = first_pull(grad_first)
    grad_branch_low = grad_resid.astype(jnp.bfloat16)
    grad_back = lax.dot_general(
        mixed_rows, grad_branch_low, contract_rows, preferred_element_type=jnp.float32
    )
    grad_mixed = (
        lax.dot_general(grad_branch_low, w_back, contract_cols, preferred_element_type=jnp.float32)
        .astype(jnp.bfloat16)
        .reshape(slot_count, block_len, local_width)
    )
    grad_queries, grad_pairs = lax.map(
        lambda slot_items: slot_grads(
            slot_items[0],
            slot_items[1],
            slot_items[2],
            slot_items[3],
            slot_items[4],
            score_scale,
            head_dim,
        ),
        (queries, key_values, lengths, grad_mixed, log_totals),
    )
    grad_proj = jnp.concatenate(
        [grad_queries.astype(jnp.bfloat16)[:, None], grad_pairs.astype(jnp.bfloat16)], axis=1
    )
    grad_w_proj = jnp.einsum(
        "sbd,spbc->pdc", hidden_in, grad_proj, preferred_element_type=jnp.float32
    )
    grad_proj_bias = jnp.stack(
        [
            jnp.sum(grad_proj[:, 0], axis=(0, 1), dtype=jnp.float32),
            jnp.sum(grad_proj[:, 2], axis=(0, 1), dtype=jnp.float32),
        ]
    ).reshape(proj_bias.shape)
    grad_tokens = jnp.einsum(
        "spbc,pdc->sbd", grad_proj, w_proj, preferred_element_type=jnp.float32
    ).reshape(token_count, model_width)
    hidden_grad = (
        (grad_resid + lax.psum(grad_tokens.astype(jnp.bfloat16), "tp").astype(jnp.float32))
        .astype(jnp.bfloat16)
        .reshape(slot_count, block_len, model_width)
    )
    grad_biases = jnp.stack(
        [
            jnp.sum(grad_branch_low, axis=0, dtype=jnp.float32),
            jnp.sum(grad_second_low, axis=0, dtype=jnp.float32),
        ]
    )
    grad_gains = jnp.stack([grad_gain_one, grad_gain_two])
    grad_shifts = jnp.stack([grad_shift_one, grad_shift_two])
    grad_up_bias = jnp.sum(grad_pre_low, axis=0, dtype=jnp.float32)
    shares = (
        lax.psum_scatter(
            grad_w_proj.astype(jnp.bfloat16), "fsdp", scatter_dimension=1, tiled=True
        ).astype(jnp.float32),
        lax.psum_scatter(
            grad_proj_bias.astype(jnp.bfloat16), "fsdp", scatter_dimension=2, tiled=True
        ).astype(jnp.float32),
        lax.psum_scatter(
            grad_back.astype(jnp.bfloat16), "fsdp", scatter_dimension=1, tiled=True
        ).astype(jnp.float32),
        lax.psum_scatter(
            grad_biases.astype(jnp.bfloat16), "fsdp", scatter_dimension=1, tiled=True
        ).astype(jnp.float32),
        lax.psum_scatter(
            grad_gains.astype(jnp.bfloat16), "fsdp", scatter_dimension=1, tiled=True
        ).astype(jnp.float32),
        lax.psum_scatter(
            grad_shifts.astype(jnp.bfloat16), "fsdp", scatter_dimension=1, tiled=True
        ).astype(jnp.float32),
        lax.psum_scatter(
            grad_up.astype(jnp.bfloat16), "fsdp", scatter_dimension=1, tiled=True
        ).astype(jnp.float32),
        lax.psum_scatter(
            grad_up_bias.astype(jnp.bfloat16), "fsdp", scatter_dimension=0, tiled=True
        ).astype(jnp.float32),
        lax.psum_scatter(
            grad_down.astype(jnp.bfloat16), "fsdp", scatter_dimension=0, tiled=True
        ).astype(jnp.float32),
    )
    owned = (
        lax.psum(shares[0].astype(jnp.bfloat16), "ctx").astype(jnp.float32),
        lax.psum(shares[1].astype(jnp.bfloat16), "ctx").astype(jnp.float32),
        lax.psum(shares[2].astype(jnp.bfloat16), "ctx").astype(jnp.float32),
        lax.psum(shares[3].astype(jnp.bfloat16), "ctx").astype(jnp.float32),
        lax.psum(shares[4].astype(jnp.bfloat16), "ctx").astype(jnp.float32),
        lax.psum(shares[5].astype(jnp.bfloat16), "ctx").astype(jnp.float32),
        lax.psum(shares[6].astype(jnp.bfloat16), "ctx").astype(jnp.float32),
        lax.psum(shares[7].astype(jnp.bfloat16), "ctx").astype(jnp.float32),
        lax.psum(shares[8].astype(jnp.bfloat16), "ctx").astype(jnp.float32),
    )
    return (
        hidden_out,
        hidden_grad,
        owned[0],
        owned[1],
        owned[2],
        owned[3],
        owned[4],
        owned[5],
        owned[6],
        owned[7],
        owned[8],
    )


def solution(mesh):
    return jax.shard_map(
        per_device,
        mesh=mesh,
        in_specs=(
            P("fsdp", "ctx", None),
            P("fsdp"),
            P("fsdp", "ctx", None),
            P(None, "fsdp", "tp"),
            P(None, "tp", "fsdp"),
            P("tp", "fsdp"),
            P(None, "fsdp"),
            P(None, "fsdp"),
            P(None, "fsdp"),
            P(None, ("fsdp", "tp")),
            P(("fsdp", "tp")),
            P(("fsdp", "tp"), None),
        ),
        out_specs=(
            P("fsdp", "ctx", None),
            P("fsdp", "ctx", None),
            P(None, "fsdp", "tp"),
            P(None, "tp", "fsdp"),
            P("tp", "fsdp"),
            P(None, "fsdp"),
            P(None, "fsdp"),
            P(None, "fsdp"),
            P(None, ("fsdp", "tp")),
            P(("fsdp", "tp")),
            P(("fsdp", "tp"), None),
        ),
        check_vma=False,
    )
```

profile of v0, /device:TPU:0, one launch (start us, length us, event | category | flops | bytes accessed | tf_op | source)
XLA Modules:
  0.0 1103.8 jit_solution(3920871484078852565)
XLA Ops:
  8.7 14.8 %all_gather.34 = bf16[2,6,64]{1,0,2:T(2,128)(2,1)S(1)} all-gather(bf16[2,6,16]{1,0,2:T(2,128)(2,1)S(1)} %copy.57), channel_id=1, replica_groups=mesh['fsdp'=4,'ctx'=4,'tp'=2] {'fsdp'}, dimensions={2}, use_global_device_ids=true | all-gather | bytes 1920 | tf_op jit(solution)/shard_map/all_gather | solution.py:125
  24.0 24.4 %all_gather.35 = bf16[384,768]{0,1:T(8,128)(2,1)S(1)} all-gather(bf16[384,192]{0,1:T(8,128)(2,1)} %param.21), channel_id=1, replica_groups=mesh['fsdp'=4,'ctx'=4,'tp'=2] {'fsdp'}, dimensions={1}, use_global_device_ids=true | all-gather | bytes 737280 | tf_op jit(solution)/shard_map/all_gather | solution.py:126
  48.5 13.6 %all-gather.16.cloned.1.call-done = bf16[3,768,384]{2,1,0:T(8,128)(2,1)} async-done(((bf16[3,192,384]{2,1,0:T(8,128)(2,1)}), bf16[3,768,384]{2,1,0:T(8,128)(2,1)}) %all-gather.16.cloned.1.call-update) | async-done | bytes 1769488 | tf_op jit(solution)/shard_map/all_gather | solution.py:124
  62.1 4.1 fusion.18
  67.7 162.6 %while.24 = (s32[]{:T(128)}, bf16[4,256,384]{2,1,0:T(8,128)(2,1)S(1)}, f32[4,6,256]{2,1,0:T(8,128)S(1)}, bf16[4,2,256,384]{2,3,1,0:T(8,128)(2,1)}, s32[4]{0:T(12...) while((s32[]{:T(128)}, bf16[4,256,384]{2,1,0:T(8,128)(2,1)S(1)}, f32[4,6,256]{2,1,0:T(8,128)S(1)}, ...), condition=%wide.region_7.8_spmd, body=%wide.region_0.7_spmd.sunk | while | flops 414353920 | bytes 35844252 | solution.py:154
  70.8 30.0 %all-gather.22.cloned.1.call-done = bf16[1,2,1024,384]{2,3,1,0:T(8,128)(2,1)} async-done(((bf16[1,2,256,384]{2,3,1,0:T(8,128)(2,1)}), bf16[1,2,1024,384]{2,3,1,0:T(8,128)(2,1)}) %all-gather.22.cloned.1.call-update) | async-done | bytes 1572880 | tf_op jit(solution)/shard_map/while/body/eval_jaxpr/all_gather | solution.py:35
  110.8 31.1 %all-gather.22.cloned.1.call-done = bf16[1,2,1024,384]{2,3,1,0:T(8,128)(2,1)} async-done(((bf16[1,2,256,384]{2,3,1,0:T(8,128)(2,1)}), bf16[1,2,1024,384]{2,3,1,0:T(8,128)(2,1)}) %all-gather.22.cloned.1.call-update) | async-done | bytes 1572880 | tf_op jit(solution)/shard_map/while/body/eval_jaxpr/all_gather | solution.py:35
  151.9 30.8 %all-gather.22.cloned.1.call-done = bf16[1,2,1024,384]{2,3,1,0:T(8,128)(2,1)} async-done(((bf16[1,2,256,384]{2,3,1,0:T(8,128)(2,1)}), bf16[1,2,1024,384]{2,3,1,0:T(8,128)(2,1)}) %all-gather.22.cloned.1.call-update) | async-done | bytes 1572880 | tf_op jit(solution)/shard_map/while/body/eval_jaxpr/all_gather | solution.py:35
  192.7 30.8 %all-gather.22.cloned.1.call-done = bf16[1,2,1024,384]{2,3,1,0:T(8,128)(2,1)} async-done(((bf16[1,2,256,384]{2,3,1,0:T(8,128)(2,1)}), bf16[1,2,1024,384]{2,3,1,0:T(8,128)(2,1)}) %all-gather.22.cloned.1.call-update) | async-done | bytes 1572880 | tf_op jit(solution)/shard_map/while/body/eval_jaxpr/all_gather | solution.py:35
  230.4 2.7 fusion.62
  234.7 10.9 all-gather.2
  245.8 7.6 all-gather.3
  253.5 9.6 all-gather.4
  263.2 12.6 %all-gather.5 = bf16[4,1,384]{2,1,0:T(2,128)(2,1)S(1)} all-gather(bf16[1,1,384]{2,1,0:T(2,128)(2,1)S(1)} %reshape.402), channel_id=1, replica_groups=mesh['fsdp'=4,'ctx'=4,'tp'=2] {'fsdp'}, dimensions={0}, use_global_device_ids=true | all-gather | bytes 3840 | tf_op jit(solution)/shard_map/all_gather | solution.py:131
  275.9 2.9 fusion.47
  279.3 30.5 %all-gather.18.cloned.1.call-done = bf16[768,1536]{1,0:T(8,128)(2,1)} async-done(((bf16[768,384]{1,0:T(8,128)(2,1)}), bf16[768,1536]{1,0:T(8,128)(2,1)}) %all-gather.18.cloned.1.call-update) | async-done | bytes 2359312 | tf_op jit(solution)/shard_map/all_gather | solution.py:130
  309.7 19.6 %multiply_convert_fusion.3 = (bf16[1024,1536]{1,0:T(8,128)(2,1)}, f32[1024,1536]{1,0:T(8,128)}, f32[1024,1536]{1,0:T(8,128)}) fusion(f32[1536]{0:T(1024)S(1)} %reshape.404, bf16[768,1536]{1,0:T(8,128)(2,1)} %all-gather.18.cloned.1.call-done, f32[1024,768]{1,0:T(8,128)S(1)} %get-tuple-element.255, f32[768]{0:T(1024)S(1)} %get-tuple-element.199, ...), kind=kOutput, calls=%fused_computation.70 | convolution fusion | flops 2523660288 | bytes 21254144 | tf_op jit(solution)/shard_map/dot_general | solution.py:172
  329.3 31.3 %all-gather.20.cloned.1.call-done = bf16[1536,768]{1,0:T(8,128)(2,1)} async-done(((bf16[384,768]{1,0:T(8,128)(2,1)}), bf16[1536,768]{1,0:T(8,128)(2,1)}) %all-gather.20.cloned.1.call-update) | async-done | bytes 2359312 | tf_op jit(solution)/shard_map/all_gather | solution.py:132
  360.6 6.9 fusion.63
  368.5 21.3 %all-reduce.11.cloned.1.call-done = f32[1024,768]{1,0:T(8,128)} async-done(((f32[1024,768]{1,0:T(8,128)}), f32[1024,768]{1,0:T(8,128)}) %all-reduce.11.cloned.1.call-update) | async-done | bytes 3145744 | tf_op jit(solution)/shard_map/psum | solution.py:177
  389.7 3.0 fusion.45
  395.8 2.8 fusion.44
  401.5 4.5 fusion.40
  407.7 4.3 fusion.64
  412.1 6.1 convolution_convert_fusion.7
  418.2 4.4 copy.86
  422.6 14.0 %all-reduce.13.cloned.1.call-done = f32[1024,768]{1,0:T(8,128)} async-done(((f32[1024,768]{1,0:T(8,128)}), f32[1024,768]{1,0:T(8,128)}) %all-reduce.13.cloned.1.call-update) | async-done | bytes 3145744 | tf_op jit(solution)/shard_map/psum | solution.py:204
  436.6 3.7 multiply_reduce_fusion.5
  444.3 306.6 %while.25 = (s32[]{:T(128)}, bf16[4,256,384]{2,1,0:T(8,128)(2,1)}, bf16[4,2,256,384]{3,2,1,0:T(8,128)(2,1)}, bf16[4,2,256,384]{2,3,1,0:T(8,128)(2,1)}, s32[4]{0:...) while((s32[]{:T(128)}, bf16[4,256,384]{2,1,0:T(8,128)(2,1)}, ...), condition=%wide.region_24.25_spmd, body=%wide.region_19.24_spmd.sunk | while | flops 1028259328 | bytes 90409344 | solution.py:217
  444.6 2.0 constant_dynamic-slice_fusion.7
  449.1 30.3 %all-gather.24.cloned.1.call-done = bf16[1,2,1024,384]{2,3,1,0:T(8,128)(2,1)} async-done(((bf16[1,2,256,384]{2,3,1,0:T(8,128)(2,1)}), bf16[1,2,1024,384]{2,3,1,0:T(8,128)(2,1)}) %all-gather.24.cloned.1.call-update) | async-done | bytes 1572880 | tf_op jit(solution)/shard_map/while/body/eval_jaxpr/all_gather | solution.py:59
  493.3 26.9 %reduce-scatter.38.cloned.1.call-done = bf16[2,256,384]{1,2,0:T(8,128)(2,1)} async-done(((bf16[2,1024,384]{1,2,0:T(8,128)(2,1)}), bf16[2,256,384]{1,2,0:T(8,128)(2,1)}) %reduce-scatter.38.cloned.1.call-update) | async-done | bytes 393232 | tf_op jit(solution)/shard_map/while/body/eval_jaxpr/reduce_scatter | solution.py:103
  522.2 2.0 constant_dynamic-slice_fusion.7
  526.7 29.1 %all-gather.24.cloned.1.call-done = bf16[1,2,1024,384]{2,3,1,0:T(8,128)(2,1)} async-done(((bf16[1,2,256,384]{2,3,1,0:T(8,128)(2,1)}), bf16[1,2,1024,384]{2,3,1,0:T(8,128)(2,1)}) %all-gather.24.cloned.1.call-update) | async-done | bytes 1572880 | tf_op jit(solution)/shard_map/while/body/eval_jaxpr/all_gather | solution.py:59
  569.7 26.9 %reduce-scatter.38.cloned.1.call-done = bf16[2,256,384]{1,2,0:T(8,128)(2,1)} async-done(((bf16[2,1024,384]{1,2,0:T(8,128)(2,1)}), bf16[2,256,384]{1,2,0:T(8,128)(2,1)}) %reduce-scatter.38.cloned.1.call-update) | async-done | bytes 393232 | tf_op jit(solution)/shard_map/while/body/eval_jaxpr/reduce_scatter | solution.py:103
  598.6 2.0 constant_dynamic-slice_fusion.7
  603.2 28.8 %all-gather.24.cloned.1.call-done = bf16[1,2,1024,384]{2,3,1,0:T(8,128)(2,1)} async-done(((bf16[1,2,256,384]{2,3,1,0:T(8,128)(2,1)}), bf16[1,2,1024,384]{2,3,1,0:T(8,128)(2,1)}) %all-gather.24.cloned.1.call-update) | async-done | bytes 1572880 | tf_op jit(solution)/shard_map/while/body/eval_jaxpr/all_gather | solution.py:59
  645.9 26.9 %reduce-scatter.38.cloned.1.call-done = bf16[2,256,384]{1,2,0:T(8,128)(2,1)} async-done(((bf16[2,1024,384]{1,2,0:T(8,128)(2,1)}), bf16[2,256,384]{1,2,0:T(8,128)(2,1)}) %reduce-scatter.38.cloned.1.call-update) | async-done | bytes 393232 | tf_op jit(solution)/shard_map/while/body/eval_jaxpr/reduce_scatter | solution.py:103
  674.8 2.0 constant_dynamic-slice_fusion.7
  679.3 28.8 %all-gather.24.cloned.1.call-done = bf16[1,2,1024,384]{2,3,1,0:T(8,128)(2,1)} async-done(((bf16[1,2,256,384]{2,3,1,0:T(8,128)(2,1)}), bf16[1,2,1024,384]{2,3,1,0:T(8,128)(2,1)}) %all-gather.24.cloned.1.call-update) | async-done | bytes 1572880 | tf_op jit(solution)/shard_map/while/body/eval_jaxpr/all_gather | solution.py:59
  722.0 26.9 %reduce-scatter.38.cloned.1.call-done = bf16[2,256,384]{1,2,0:T(8,128)(2,1)} async-done(((bf16[2,1024,384]{1,2,0:T(8,128)(2,1)}), bf16[2,256,384]{1,2,0:T(8,128)(2,1)}) %reduce-scatter.38.cloned.1.call-update) | async-done | bytes 393232 | tf_op jit(solution)/shard_map/while/body/eval_jaxpr/reduce_scatter | solution.py:103
  751.7 5.4 fusion.23
  757.1 4.0 copy.76
  762.8 3.4 convolution_convert_fusion.9
  766.5 6.0 convolution_convert_fusion.6
  779.9 5.4 bitcast_convert_fusion.2
  785.3 16.9 %reduce-scatter.36.cloned.1.call-done = bf16[384,768]{1,0:T(8,128)(2,1)} async-done(((bf16[1536,768]{1,0:T(8,128)(2,1)}), bf16[384,768]{1,0:T(8,128)(2,1)}) %reduce-scatter.36.cloned.1.call-update) | async-done | bytes 589840
  802.2 2.1 copy.87
  804.3 38.1 %reduce-scatter.26.cloned.1.call-done = bf16[192,1152]{1,0:T(8,128)(2,1)} async-done(((bf16[768,1152]{1,0:T(8,128)(2,1)}), bf16[192,1152]{1,0:T(8,128)(2,1)}) %reduce-scatter.26.cloned.1.call-update) | async-done | bytes 442384
  842.4 2.1 reshape.410
  844.5 2.1 copy.77
  846.6 19.7 %reduce-scatter.22.cloned.1.call-done = bf16[384,192]{0,1:T(8,128)(2,1)} async-done(((bf16[384,768]{0,1:T(8,128)(2,1)}), bf16[384,192]{0,1:T(8,128)(2,1)}) %reduce-scatter.22.cloned.1.call-update) | async-done | bytes 147472 | tf_op jit(solution)/shard_map/reduce_scatter | solution.py:265
  866.4 48.7 %reduce-scatter.24.cloned.1.call-done = bf16[384,768]{1,0:T(8,128)(2,1)} async-done(((bf16[1536,768]{1,0:T(8,128)(2,1)}), bf16[384,768]{1,0:T(8,128)(2,1)}) %reduce-scatter.24.cloned.1.call-update) | async-done | bytes 589840 | tf_op jit(solution)/shard_map/reduce_scatter | solution.py:283
  916.3 9.9 all-reduce
  926.4 9.4 reduce-scatter.28.cloned.1.call-done
  936.6 18.9 %reduce-scatter.32.cloned.1.call-done = bf16[192,2]{1,0:T(8,128)(2,1)} async-done(((bf16[768,2]{1,0:T(8,128)(2,1)}), bf16[192,2]{1,0:T(8,128)(2,1)}) %reduce-scatter.32.cloned.1.call-update) | async-done | bytes 784
  956.3 19.6 %reduce-scatter.30.cloned.1.call-done = bf16[192,2]{1,0:T(8,128)(2,1)} async-done(((bf16[768,2]{1,0:T(8,128)(2,1)}), bf16[192,2]{1,0:T(8,128)(2,1)}) %reduce-scatter.30.cloned.1.call-update) | async-done | bytes 784
  976.8 18.9 %reduce-scatter.34.cloned.1.call-done = bf16[192,2]{1,0:T(8,128)(2,1)} async-done(((bf16[768,2]{1,0:T(8,128)(2,1)}), bf16[192,2]{1,0:T(8,128)(2,1)}) %reduce-scatter.34.cloned.1.call-update) | async-done | bytes 784
  996.6 10.0 all-reduce.1
  1009.5 7.6 all-reduce.15.cloned.1.call-done
  1017.1 3.0 add_convert_fusion.2
  1020.1 70.2 %all-reduce.17.cloned.1.call-done = (bf16[3,192,384]{1,2,0:T(8,128)(2,1)}, bf16[384,192]{0,1:T(8,128)(2,1)}, bf16[768,384]{1,0:T(8,128)(2,1)}, bf16[384,768]{1,0:T(8,128)(2,1)}) async-done(((bf16[3,192,384]{1,2,0:T(8,128)(2,1)}, bf16[384,192]{0,1:T(8,128)(2,1)}, bf16[768,384]{1,0:T(8,128)(2,1)}, bf16[384,768]{1,0:T(8,128)(2,1)}), (bf16[3,192,384]{1,2,0:T(8,128)(2,1)}, bf16[384,192]{0,1:T(8,128)(2,1)}, ...) | async-done | bytes 1769488 | tf_op jit(solution)/shard_map/psum | solution.py:288
  1090.3 2.2 convert_element_type.272
  1092.5 2.2 convert_element_type.275
  (469 shorter events, 149.5 us)
Async XLA Ops:
  7.2 54.9 %all-gather.16.cloned.1.call-start = ((), (), s32[]{:S(2)}) async-start(), calls=%async_computation.9 | async-start | bytes 2211840 | tf_op jit(solution)/shard_map/all_gather | solution.py:124
  48.4 182.0 %copy-start.8 = (bf16[384,768]{0,1:T(8,128)(2,1)}, bf16[384,768]{0,1:T(8,128)(2,1)S(1)}, u32[]{:S(2)}) copy-start(bf16[384,768]{0,1:T(8,128)(2,1)S(1)} %all_gather.35) | copy-start | bytes 1769476
  67.7 33.1 %all-gather.22.cloned.1.call-start = ((), (), s32[]{:S(2)}) async-start(), calls=%async_computation.25 | async-start | bytes 1966080 | tf_op jit(solution)/shard_map/while/body/eval_jaxpr/all_gather | solution.py:35
  107.7 34.3 %all-gather.22.cloned.1.call-start = ((), (), s32[]{:S(2)}) async-start(), calls=%async_computation.25 | async-start | bytes 1966080 | tf_op jit(solution)/shard_map/while/body/eval_jaxpr/all_gather | solution.py:35
  148.8 33.9 %all-gather.22.cloned.1.call-start = ((), (), s32[]{:S(2)}) async-start(), calls=%async_computation.25 | async-start | bytes 1966080 | tf_op jit(solution)/shard_map/while/body/eval_jaxpr/all_gather | solution.py:35
  189.5 33.9 %all-gather.22.cloned.1.call-start = ((), (), s32[]{:S(2)}) async-start(), calls=%async_computation.25 | async-start | bytes 1966080 | tf_op jit(solution)/shard_map/while/body/eval_jaxpr/all_gather | solution.py:35
  230.3 2.8 copy-start.7
  230.3 2.8 copy-start.16
  230.4 45.5 %all-reduce.9.cloned.1.call-start = ((), (), s32[]{:S(2)}) async-start(), calls=%async_computation.10 | async-start | bytes 6291456 | tf_op jit(solution)/shard_map/psum | solution.py:162
  233.1 12.6 %copy-start.22 = (bf16[2,192]{1,0:T(2,128)(2,1)S(1)}, bf16[2,192]{1,0:T(2,128)(2,1)}, u32[]{:S(2)}) copy-start(bf16[2,192]{1,0:T(2,128)(2,1)} %param.23) | copy-start | bytes 2308
  233.1 20.3 %copy-start.23 = (bf16[2,192]{1,0:T(2,128)(2,1)S(1)}, bf16[2,192]{1,0:T(2,128)(2,1)}, u32[]{:S(2)}) copy-start(bf16[2,192]{1,0:T(2,128)(2,1)} %param.24) | copy-start | bytes 2308
  233.1 30.1 %copy-start.24 = (bf16[384]{0:T(512)(128)(2,1)S(1)}, bf16[384]{0:T(512)(128)(2,1)}, u32[]{:S(2)}) copy-start(bf16[384]{0:T(512)(128)(2,1)} %param.26) | copy-start | bytes 2308
  233.2 76.5 %all-gather.18.cloned.1.call-start = ((), (), s32[]{:S(2)}) async-start(), calls=%async_computation.11 | async-start | bytes 2949120 | tf_op jit(solution)/shard_map/all_gather | solution.py:130
  233.9 126.7 %all-gather.20.cloned.1.call-start = ((), (), s32[]{:S(2)}) async-start(), calls=%async_computation.12 | async-start | bytes 2949120 | tf_op jit(solution)/shard_map/all_gather | solution.py:132
  234.7 155.0 %all-reduce.11.cloned.1.call-start = ((), (), s32[]{:S(2)}) async-start(), calls=%async_computation.13 | async-start | bytes 6291456 | tf_op jit(solution)/shard_map/psum | solution.py:177
  367.6 69.1 %all-reduce.13.cloned.1.call-start = ((), (), s32[]{:S(2)}) async-start(), calls=%async_computation.14 | async-start | bytes 6291456 | tf_op jit(solution)/shard_map/psum | solution.py:204
  389.7 10.9 slice-start.2
  394.2 6.4 slice-start.3
  395.8 4.8 slice-start
  395.8 4.8 slice-start.1
  398.6 2.9 copy-start.27
  400.6 5.5 copy-start.10
  401.5 6.2 copy-start.26
  406.0 1.7 copy-start.29
  441.8 2.5 copy-start.3
  442.2 2.1 copy-start.12
  444.5 36.4 %copy-start.13 = (bf16[4,256,384]{2,1,0:T(8,128)(2,1)}, bf16[4,256,384]{2,1,0:T(8,128)(2,1)S(1)}, u32[]{:S(2)}) copy-start(bf16[4,256,384]{2,1,0:T(8,128)(2,1)S(1)} %get-tuple-element.526) | copy-start | bytes 2359300 | tf_op jit(solution)/shard_map/while
  444.6 34.8 %all-gather.24.cloned.1.call-start = ((), (), s32[]{:S(2)}) async-start(), calls=%async_computation.26 | async-start | bytes 1966080 | tf_op jit(solution)/shard_map/while/body/eval_jaxpr/all_gather | solution.py:59
  446.6 73.5 %reduce-scatter.38.cloned.1.call-start = ((), (), s32[]{:S(2)}) async-start(), calls=%async_computation.27 | async-start | bytes 1966080 | tf_op jit(solution)/shard_map/while/body/eval_jaxpr/reduce_scatter | solution.py:103
  481.0 2.7 copy-start
  490.5 31.7 %copy-start.14 = (bf16[4,256,384]{2,1,0:T(8,128)(2,1)S(1)}, bf16[4,256,384]{2,1,0:T(8,128)(2,1)}, u32[]{:S(2)}) copy-start(bf16[4,256,384]{2,1,0:T(8,128)(2,1)} %copy-done.13) | copy-start | bytes 2359300 | tf_op jit(solution)/shard_map/while
  522.2 35.2 %copy-start.13 = (bf16[4,256,384]{2,1,0:T(8,128)(2,1)}, bf16[4,256,384]{2,1,0:T(8,128)(2,1)S(1)}, u32[]{:S(2)}) copy-start(bf16[4,256,384]{2,1,0:T(8,128)(2,1)S(1)} %get-tuple-element.526) | copy-start | bytes 2359300 | tf_op jit(solution)/shard_map/while
  522.2 33.7 %all-gather.24.cloned.1.call-start = ((), (), s32[]{:S(2)}) async-start(), calls=%async_computation.26 | async-start | bytes 1966080 | tf_op jit(solution)/shard_map/while/body/eval_jaxpr/all_gather | solution.py:59
  524.2 72.4 %reduce-scatter.38.cloned.1.call-start = ((), (), s32[]{:S(2)}) async-start(), calls=%async_computation.27 | async-start | bytes 1966080 | tf_op jit(solution)/shard_map/while/body/eval_jaxpr/reduce_scatter | solution.py:103
  557.5 2.7 copy-start
  566.9 31.7 %copy-start.14 = (bf16[4,256,384]{2,1,0:T(8,128)(2,1)S(1)}, bf16[4,256,384]{2,1,0:T(8,128)(2,1)}, u32[]{:S(2)}) copy-start(bf16[4,256,384]{2,1,0:T(8,128)(2,1)} %copy-done.13) | copy-start | bytes 2359300 | tf_op jit(solution)/shard_map/while
  598.6 34.8 %copy-start.13 = (bf16[4,256,384]{2,1,0:T(8,128)(2,1)}, bf16[4,256,384]{2,1,0:T(8,128)(2,1)S(1)}, u32[]{:S(2)}) copy-start(bf16[4,256,384]{2,1,0:T(8,128)(2,1)S(1)} %get-tuple-element.526) | copy-start | bytes 2359300 | tf_op jit(solution)/shard_map/while
  598.6 33.3 %all-gather.24.cloned.1.call-start = ((), (), s32[]{:S(2)}) async-start(), calls=%async_computation.26 | async-start | bytes 1966080 | tf_op jit(solution)/shard_map/while/body/eval_jaxpr/all_gather | solution.py:59
  600.7 72.1 %reduce-scatter.38.cloned.1.call-start = ((), (), s32[]{:S(2)}) async-start(), calls=%async_computation.27 | async-start | bytes 1966080 | tf_op jit(solution)/shard_map/while/body/eval_jaxpr/reduce_scatter | solution.py:103
  633.6 2.7 copy-start
  643.0 31.7 %copy-start.14 = (bf16[4,256,384]{2,1,0:T(8,128)(2,1)S(1)}, bf16[4,256,384]{2,1,0:T(8,128)(2,1)}, u32[]{:S(2)}) copy-start(bf16[4,256,384]{2,1,0:T(8,128)(2,1)} %copy-done.13) | copy-start | bytes 2359300 | tf_op jit(solution)/shard_map/while
  674.8 34.8 %copy-start.13 = (bf16[4,256,384]{2,1,0:T(8,128)(2,1)}, bf16[4,256,384]{2,1,0:T(8,128)(2,1)S(1)}, u32[]{:S(2)}) copy-start(bf16[4,256,384]{2,1,0:T(8,128)(2,1)S(1)} %get-tuple-element.526) | copy-start | bytes 2359300 | tf_op jit(solution)/shard_map/while
  674.8 33.3 %all-gather.24.cloned.1.call-start = ((), (), s32[]{:S(2)}) async-start(), calls=%async_computation.26 | async-start | bytes 1966080 | tf_op jit(solution)/shard_map/while/body/eval_jaxpr/all_gather | solution.py:59
  676.8 72.1 %reduce-scatter.38.cloned.1.call-start = ((), (), s32[]{:S(2)}) async-start(), calls=%async_computation.27 | async-start | bytes 1966080 | tf_op jit(solution)/shard_map/while/body/eval_jaxpr/reduce_scatter | solution.py:103
  709.7 2.7 copy-start
  719.2 31.7 %copy-start.14 = (bf16[4,256,384]{2,1,0:T(8,128)(2,1)S(1)}, bf16[4,256,384]{2,1,0:T(8,128)(2,1)}, u32[]{:S(2)}) copy-start(bf16[4,256,384]{2,1,0:T(8,128)(2,1)} %copy-done.13) | copy-start | bytes 2359300 | tf_op jit(solution)/shard_map/while
  750.9 51.3 %reduce-scatter.36.cloned.1.call-start = ((), (), s32[]{:S(2)}) async-start(), calls=%async_computation.23 | async-start | bytes 2949120
  751.6 90.7 %reduce-scatter.26.cloned.1.call-start = ((), (), s32[]{:S(2)}) async-start(), calls=%async_computation.18 | async-start | bytes 2211840
  761.2 1.7 copy-start.17
  762.8 3.8 copy-start.11
  762.8 103.6 %reduce-scatter.22.cloned.1.call-start = ((), (), s32[]{:S(2)}) async-start(), calls=%async_computation.16 | async-start | bytes 737280 | tf_op jit(solution)/shard_map/reduce_scatter | solution.py:265
  766.2 6.5 copy-start.20
  766.2 148.8 %reduce-scatter.24.cloned.1.call-start = ((), (), s32[]{:S(2)}) async-start(), calls=%async_computation.17 | async-start | bytes 2949120 | tf_op jit(solution)/shard_map/reduce_scatter | solution.py:283
  772.6 1.9 copy-start.15
  772.6 163.1 %reduce-scatter.28.cloned.1.call-start = ((), (), s32[]{:S(2)}) async-start(), calls=%async_computation.19 | async-start | bytes 20480
  777.0 178.5 %reduce-scatter.32.cloned.1.call-start = ((), (), s32[]{:S(2)}) async-start(), calls=%async_computation.21 | async-start | bytes 245760
  777.9 198.0 %reduce-scatter.30.cloned.1.call-start = ((), (), s32[]{:S(2)}) async-start(), calls=%async_computation.20 | async-start | bytes 245760
  778.9 216.8 %reduce-scatter.34.cloned.1.call-start = ((), (), s32[]{:S(2)}) async-start(), calls=%async_computation.22 | async-start | bytes 245760
  779.8 237.3 %all-reduce.15.cloned.1.call-start = ((), (), s32[]{:S(2)}) async-start(), calls=%async_computation.15 | async-start | bytes 3145728 | tf_op jit(solution)/shard_map/psum | solution.py:245
  785.2 129.9 %copy-start.28 = (u32[32]{0:T(128)S(1)}, u32[32]{0:T(128)}, u32[]{:S(2)}) copy-start(u32[32]{0:T(128)} %constant.143) | copy-start | bytes 388
  785.2 231.9 %copy-start.4 = (f32[1024,768]{1,0:T(8,128)S(1)}, f32[1024,768]{1,0:T(8,128)}, u32[]{:S(2)}) copy-start(f32[1024,768]{1,0:T(8,128)} %copy-done.3) | copy-start | bytes 9437188
  785.3 305.0 %all-reduce.17.cloned.1.call-start = ((), (), s32[]{:S(2)}) async-start(), calls=%async_computation.24 | async-start | bytes 3833856 | tf_op jit(solution)/shard_map/psum | solution.py:288
  1090.3 4.4 copy-start.18
  1090.3 5.5 copy-start.19
  (10 other events, 14.2 us)
Sparse Core Ops, SparseCore 0:
  9.6 52.4 all-gather.15
  71.1 29.6 all-gather.21
  111.0 30.8 all-gather.21
  151.8 30.8 all-gather.21
  192.6 30.8 all-gather.21
  233.3 23.1 all-reduce.8
  258.2 51.4 all-gather.17
  311.4 49.2 all-gather.19
  367.7 22.0 all-reduce.10
  412.2 24.3 all-reduce.12
  447.4 31.9 all-gather.23
  489.2 30.9 reduce-scatter.37
  525.0 30.8 all-gather.23
  565.6 30.9 reduce-scatter.37
  601.1 30.7 all-gather.23
  641.8 30.9 reduce-scatter.37
  677.2 30.7 all-gather.23
  717.9 30.9 reduce-scatter.37
  754.1 47.9 reduce-scatter.35
  804.5 37.8 reduce-scatter.25
  845.2 21.0 reduce-scatter.21
  868.7 46.3 reduce-scatter.23
  917.3 18.3 reduce-scatter.27
  937.9 17.4 reduce-scatter.31
  958.3 17.6 reduce-scatter.29
  978.1 17.5 reduce-scatter.33
  998.5 18.6 all-reduce.14
  1021.6 68.6 all-reduce.16
where the time goes:
time: 1110 us; the launch traced here: 1100 us
  waiting for transfers between devices  729 us (66%)
  matrix products  119 us (11%)
  blocking collectives  99.8 us (9%)
  local copies, waits for them, and re-layouts  86.6 us (8%)
  other arithmetic  50.7 us (5%)
  between operations  16 us (1%)
    unnamed x22, waiting for transfers between devices  125 us
    all_gather x4, waiting for transfers between devices, attend_slot(): gathered = lax.all_gather(key_value, 'ctx', axis=1, tiled=True)  123 us
    all_gather x4, waiting for transfers between devices, slot_grads(): gathered = lax.all_gather(key_value, 'ctx', axis=1, tiled=True)  117 us
    reduce_scatter x4, waiting for transfers between devices, slot_grads(): lax.psum_scatter(key_terms.astype(jnp.bfloat16), 'ctx', scatter_dimension...  108 us
    psum x1, waiting for transfers between devices, per_device(): lax.psum(shares[0].astype(jnp.bfloat16), 'ctx').astype(jnp.float32)  70.2 us
    reduce_scatter x1, waiting for transfers between devices, per_device(): lax.psum_scatter(grad_down.astype(jnp.bfloat16), 'fsdp', scatter_dimensio...  48.7 us
    unnamed x88, local copies, waits for them, and re-layouts  34.5 us
    all_gather x1, waiting for transfers between devices, per_device(): lax.all_gather(w_ffo, 'fsdp', axis=0, tiled=True)  31.3 us
  transfers between devices with their start and end apart: 28, of which 27 were waited for; matrix products, arithmetic and copies ran while one was open for 10% of the time, Pallas kernels for 0%

commit v1 on v0

--- a/solution.py
+++ b/solution.py
@@ -32,7 +32,14 @@
 
 
 def attend_slot(queries, key_value, length, score_scale, head_dim):
-    gathered = lax.all_gather(key_value, "ctx", axis=1, tiled=True)
+    ways, here, step = (lax.axis_size("ctx"), lax.axis_index("ctx"), key_value.shape[1])
+    line, have = (key_value, 1)
+    while have < ways:
+        line = jnp.concatenate(
+            [line, lax.ppermute(line, "ctx", [(d, (d - have) % ways) for d in range(ways)])], axis=1
+        )
+        have = 2 * have
+    gathered = jnp.roll(line, here * step, axis=1)
     seq_len = gathered.shape[1]
     key_mask = lax.iota(jnp.int32, seq_len) < length
     block_width = heads_together * head_dim

time: 1110 us -> 1110 us (level)
  waiting for transfers between devices: 729 us -> 687 us
  local copies, waits for them, and re-layouts: 86.6 us -> 107 us
  starting transfers between devices: 1.41 us -> 20.6 us
    all_gather x4 -> x0, waiting for transfers between devices: 123 us -> none  [attend_slot(): gathered = lax.all_gather(key_value, 'ctx', axis=1, tiled=True)]
    ppermute x0 -> x8, waiting for transfers between devices: none -> 77.1 us  [attend_slot(): lax.ppermute(line, 'ctx', [(d, (d - have) % ways) for d in range(ways)])]
    while x32 -> x52, local copies, waits for them, and re-layouts: 0.07 us -> 21.1 us
    ppermute x0 -> x8, starting transfers between devices: none -> 19.3 us  [attend_slot(): lax.ppermute(line, 'ctx', [(d, (d - have) % ways) for d in range(ways)])]
    unnamed x88 -> x84, local copies, waits for them, and re-layouts: 34.5 us -> 34.5 us
  transfers between devices with their start and end apart: 28 -> 32, of which waited for: 27 -> 31; matrix products, arithmetic and copies ran while one was open for 10% -> 11% of each run, Pallas kernels for 0% -> 0%
where the time goes in v1:
time: 1110 us; the launch traced here: 1100 us
  waiting for transfers between devices  687 us (62%)
  matrix products  120 us (11%)
  local copies, waits for them, and re-layouts  107 us (10%)
  blocking collectives  98.8 us (9%)
  other arithmetic  50.9 us (5%)
  starting transfers between devices  20.6 us (2%)
  between operations  16 us (1%)
    unnamed x22, waiting for transfers between devices  124 us
    all_gather x4, waiting for transfers between devices, slot_grads(): gathered = lax.all_gather(key_value, 'ctx', axis=1, tiled=True)  118 us
    reduce_scatter x4, waiting for transfers between devices, slot_grads(): lax.psum_scatter(key_terms.astype(jnp.bfloat16), 'ctx', scatter_dimension...  108 us
    ppermute x8, waiting for transfers between devices, attend_slot(): lax.ppermute(line, 'ctx', [(d, (d - have) % ways) for d in range(ways)])  77.1 us
    psum x1, waiting for transfers between devices, per_device(): lax.psum(shares[0].astype(jnp.bfloat16), 'ctx').astype(jnp.float32)  70 us
    reduce_scatter x1, waiting for transfers between devices, per_device(): lax.psum_scatter(grad_down.astype(jnp.bfloat16), 'fsdp', scatter_dimensio...  48.5 us
    all_gather x1, waiting for transfers between devices, per_device(): lax.all_gather(w_in, 'fsdp', axis=1, tiled=True)  34.6 us
    unnamed x84, local copies, waits for them, and re-layouts  34.5 us
  transfers between devices with their start and end apart: 32, of which 31 were waited for; matrix products, arithmetic and copies ran while one was open for 11% of the time, Pallas kernels for 0%

profile of v1, /device:TPU:0, one launch (start us, length us, event | category | flops | bytes accessed | tf_op | source)
XLA Modules:
  0.0 1101.8 jit_solution(4061136415342956548)
XLA Ops:
  8.8 14.8 %all_gather.31 = bf16[2,6,64]{1,0,2:T(2,128)(2,1)S(1)} all-gather(bf16[2,6,16]{1,0,2:T(2,128)(2,1)S(1)} %copy.57), channel_id=1, replica_groups=mesh['fsdp'=4,'ctx'=4,'tp'=2] {'fsdp'}, dimensions={2}, use_global_device_ids=true | all-gather | bytes 1920 | tf_op jit(solution)/shard_map/all_gather | solution.py:132
  24.1 24.9 %all_gather.32 = bf16[384,768]{0,1:T(8,128)(2,1)} all-gather(bf16[384,192]{0,1:T(8,128)(2,1)} %param.21), channel_id=1, replica_groups=mesh['fsdp'=4,'ctx'=4,'tp'=2] {'fsdp'}, dimensions={1}, use_global_device_ids=true | all-gather | bytes 737280 | tf_op jit(solution)/shard_map/all_gather | solution.py:133
  49.0 13.1 %all-gather.12.cloned.1.call-done = bf16[3,768,384]{2,1,0:T(8,128)(2,1)} async-done(((bf16[3,192,384]{2,1,0:T(8,128)(2,1)}), bf16[3,768,384]{2,1,0:T(8,128)(2,1)}) %all-gather.12.cloned.1.call-update) | async-done | bytes 1769488 | tf_op jit(solution)/shard_map/all_gather | solution.py:131
  62.1 4.1 fusion.18
  67.7 156.7 %while.26 = (s32[]{:T(128)}, bf16[4,256,384]{2,1,0:T(8,128)(2,1)}, f32[4,6,256]{2,1,0:T(8,128)S(1)}, bf16[4,2,256,384]{2,3,1,0:T(8,128)(2,1)}, s32[4]{0:T(128)S(...) while((s32[]{:T(128)}, bf16[4,256,384]{2,1,0:T(8,128)(2,1)}, ...), condition=%wide.region_7.8_spmd, body=%wide.region_0.7_spmd.sunk | while | flops 415926816 | bytes 42136032 | solution.py:161
  69.5 2.4 collective-permute-start
  71.9 8.4 collective-permute-done
  84.1 14.8 %collective-permute-done.1 = bf16[2,512,384]{1,2,0:T(8,128)(2,1)S(1)} collective-permute-done((bf16[2,512,384]{1,2,0:T(8,128)(2,1)S(1)}, bf16[2,512,384]{1,2,0:T(8,128)(2,1)S(1)}, u32[]{:S(2)}, u32[]{:S(2)}) %collective-permute-start.1) | collective-permute-done | bytes 786464 | tf_op jit(solution)/shard_map/while/body/eval_jaxpr/ppermute | solution.py:39
  111.7 3.3 collective-permute-start
  115.0 6.5 collective-permute-done
  125.1 13.2 %collective-permute-done.1 = bf16[2,512,384]{1,2,0:T(8,128)(2,1)S(1)} collective-permute-done((bf16[2,512,384]{1,2,0:T(8,128)(2,1)S(1)}, bf16[2,512,384]{1,2,0:T(8,128)(2,1)S(1)}, u32[]{:S(2)}, u32[]{:S(2)}) %collective-permute-start.1) | collective-permute-done | bytes 786464 | tf_op jit(solution)/shard_map/while/body/eval_jaxpr/ppermute | solution.py:39
  151.2 3.5 collective-permute-start
  154.7 5.3 collective-permute-done
  163.2 11.8 %collective-permute-done.1 = bf16[2,512,384]{1,2,0:T(8,128)(2,1)S(1)} collective-permute-done((bf16[2,512,384]{1,2,0:T(8,128)(2,1)S(1)}, bf16[2,512,384]{1,2,0:T(8,128)(2,1)S(1)}, u32[]{:S(2)}, u32[]{:S(2)}) %collective-permute-start.1) | collective-permute-done | bytes 786464 | tf_op jit(solution)/shard_map/while/body/eval_jaxpr/ppermute | solution.py:39
  187.9 5.2 collective-permute-start
  193.1 5.3 collective-permute-done
  201.7 11.7 %collective-permute-done.1 = bf16[2,512,384]{1,2,0:T(8,128)(2,1)S(1)} collective-permute-done((bf16[2,512,384]{1,2,0:T(8,128)(2,1)S(1)}, bf16[2,512,384]{1,2,0:T(8,128)(2,1)S(1)}, u32[]{:S(2)}, u32[]{:S(2)}) %collective-permute-start.1) | collective-permute-done | bytes 786464 | tf_op jit(solution)/shard_map/while/body/eval_jaxpr/ppermute | solution.py:39
  224.4 4.3 fusion.62
  230.1 9.5 all-gather.1
  239.7 7.7 all-gather.2
  247.6 9.5 all-gather.3
  257.2 12.5 %all-gather.4 = bf16[4,1,384]{2,1,0:T(2,128)(2,1)S(1)} all-gather(bf16[1,1,384]{2,1,0:T(2,128)(2,1)S(1)} %reshape.439), channel_id=1, replica_groups=mesh['fsdp'=4,'ctx'=4,'tp'=2] {'fsdp'}, dimensions={0}, use_global_device_ids=true | all-gather | bytes 3840 | tf_op jit(solution)/shard_map/all_gather | solution.py:138
  269.7 2.8 fusion.47
  273.1 34.6 %all-gather.14.cloned.1.call-done = bf16[768,1536]{1,0:T(8,128)(2,1)} async-done(((bf16[768,384]{1,0:T(8,128)(2,1)}), bf16[768,1536]{1,0:T(8,128)(2,1)}) %all-gather.14.cloned.1.call-update) | async-done | bytes 2359312 | tf_op jit(solution)/shard_map/all_gather | solution.py:137
  307.7 19.5 %multiply_convert_fusion.3 = (bf16[1024,1536]{1,0:T(8,128)(2,1)}, f32[1024,1536]{1,0:T(8,128)}, f32[1024,1536]{1,0:T(8,128)}) fusion(f32[1536]{0:T(1024)S(1)} %reshape.441, bf16[768,1536]{1,0:T(8,128)(2,1)} %all-gather.14.cloned.1.call-done, f32[1024,768]{1,0:T(8,128)S(1)} %get-tuple-element.304, f32[768]{0:T(1024)S(1)} %get-tuple-element.246, ...), kind=kOutput, calls=%fused_computation.77 | convolution fusion | flops 2523660288 | bytes 21254144 | tf_op jit(solution)/shard_map/dot_general | solution.py:179
  327.3 31.2 %all-gather.16.cloned.1.call-done = bf16[1536,768]{1,0:T(8,128)(2,1)} async-done(((bf16[384,768]{1,0:T(8,128)(2,1)}), bf16[1536,768]{1,0:T(8,128)(2,1)}) %all-gather.16.cloned.1.call-update) | async-done | bytes 2359312 | tf_op jit(solution)/shard_map/all_gather | solution.py:139
  358.5 6.9 fusion.63
  366.3 21.3 %all-reduce.11.cloned.1.call-done = f32[1024,768]{1,0:T(8,128)} async-done(((f32[1024,768]{1,0:T(8,128)}), f32[1024,768]{1,0:T(8,128)}) %all-reduce.11.cloned.1.call-update) | async-done | bytes 3145744 | tf_op jit(solution)/shard_map/psum | solution.py:184
  387.6 3.0 fusion.45
  393.6 2.8 fusion.44
  399.3 4.5 fusion.40
  405.6 4.3 fusion.64
  409.9 6.1 convolution_convert_fusion.7
  416.1 4.4 copy.86
  420.4 14.0 %all-reduce.13.cloned.1.call-done = f32[1024,768]{1,0:T(8,128)} async-done(((f32[1024,768]{1,0:T(8,128)}), f32[1024,768]{1,0:T(8,128)}) %all-reduce.13.cloned.1.call-update) | async-done | bytes 3145744 | tf_op jit(solution)/shard_map/psum | solution.py:211
  434.5 3.7 multiply_reduce_fusion.5
  442.2 307.2 %while.27 = (s32[]{:T(128)}, bf16[4,256,384]{2,1,0:T(8,128)(2,1)}, bf16[4,2,256,384]{3,2,1,0:T(8,128)(2,1)}, bf16[4,2,256,384]{2,3,1,0:T(8,128)(2,1)}, s32[4]{0:...) while((s32[]{:T(128)}, bf16[4,256,384]{2,1,0:T(8,128)(2,1)}, ...), condition=%wide.region_24.25_spmd, body=%wide.region_19.24_spmd.sunk | while | flops 1028259328 | bytes 90409344 | solution.py:224
  447.0 30.3 %all-gather.18.cloned.1.call-done = bf16[1,2,1024,384]{2,3,1,0:T(8,128)(2,1)} async-done(((bf16[1,2,256,384]{2,3,1,0:T(8,128)(2,1)}), bf16[1,2,1024,384]{2,3,1,0:T(8,128)(2,1)}) %all-gather.18.cloned.1.call-update) | async-done | bytes 1572880 | tf_op jit(solution)/shard_map/while/body/eval_jaxpr/all_gather | solution.py:66
  491.2 26.9 %reduce-scatter.38.cloned.1.call-done = bf16[2,256,384]{1,2,0:T(8,128)(2,1)} async-done(((bf16[2,1024,384]{1,2,0:T(8,128)(2,1)}), bf16[2,256,384]{1,2,0:T(8,128)(2,1)}) %reduce-scatter.38.cloned.1.call-update) | async-done | bytes 393232 | tf_op jit(solution)/shard_map/while/body/eval_jaxpr/reduce_scatter | solution.py:110
  524.6 29.1 %all-gather.18.cloned.1.call-done = bf16[1,2,1024,384]{2,3,1,0:T(8,128)(2,1)} async-done(((bf16[1,2,256,384]{2,3,1,0:T(8,128)(2,1)}), bf16[1,2,1024,384]{2,3,1,0:T(8,128)(2,1)}) %all-gather.18.cloned.1.call-update) | async-done | bytes 1572880 | tf_op jit(solution)/shard_map/while/body/eval_jaxpr/all_gather | solution.py:66
  567.6 26.9 %reduce-scatter.38.cloned.1.call-done = bf16[2,256,384]{1,2,0:T(8,128)(2,1)} async-done(((bf16[2,1024,384]{1,2,0:T(8,128)(2,1)}), bf16[2,256,384]{1,2,0:T(8,128)(2,1)}) %reduce-scatter.38.cloned.1.call-update) | async-done | bytes 393232 | tf_op jit(solution)/shard_map/while/body/eval_jaxpr/reduce_scatter | solution.py:110
  601.0 29.1 %all-gather.18.cloned.1.call-done = bf16[1,2,1024,384]{2,3,1,0:T(8,128)(2,1)} async-done(((bf16[1,2,256,384]{2,3,1,0:T(8,128)(2,1)}), bf16[1,2,1024,384]{2,3,1,0:T(8,128)(2,1)}) %all-gather.18.cloned.1.call-update) | async-done | bytes 1572880 | tf_op jit(solution)/shard_map/while/body/eval_jaxpr/all_gather | solution.py:66
  644.0 26.9 %reduce-scatter.38.cloned.1.call-done = bf16[2,256,384]{1,2,0:T(8,128)(2,1)} async-done(((bf16[2,1024,384]{1,2,0:T(8,128)(2,1)}), bf16[2,256,384]{1,2,0:T(8,128)(2,1)}) %reduce-scatter.38.cloned.1.call-update) | async-done | bytes 393232 | tf_op jit(solution)/shard_map/while/body/eval_jaxpr/reduce_scatter | solution.py:110
  677.5 29.1 %all-gather.18.cloned.1.call-done = bf16[1,2,1024,384]{2,3,1,0:T(8,128)(2,1)} async-done(((bf16[1,2,256,384]{2,3,1,0:T(8,128)(2,1)}), bf16[1,2,1024,384]{2,3,1,0:T(8,128)(2,1)}) %all-gather.18.cloned.1.call-update) | async-done | bytes 1572880 | tf_op jit(solution)/shard_map/while/body/eval_jaxpr/all_gather | solution.py:66
  720.4 26.9 %reduce-scatter.38.cloned.1.call-done = bf16[2,256,384]{1,2,0:T(8,128)(2,1)} async-done(((bf16[2,1024,384]{1,2,0:T(8,128)(2,1)}), bf16[2,256,384]{1,2,0:T(8,128)(2,1)}) %reduce-scatter.38.cloned.1.call-update) | async-done | bytes 393232 | tf_op jit(solution)/shard_map/while/body/eval_jaxpr/reduce_scatter | solution.py:110
  750.0 5.4 fusion.23
  755.4 4.0 copy.76
  761.1 3.4 convolution_convert_fusion.9
  764.8 6.0 convolution_convert_fusion.6
  778.1 5.4 bitcast_convert_fusion.2
  783.6 16.8 %reduce-scatter.36.cloned.1.call-done = bf16[384,768]{1,0:T(8,128)(2,1)} async-done(((bf16[1536,768]{1,0:T(8,128)(2,1)}), bf16[384,768]{1,0:T(8,128)(2,1)}) %reduce-scatter.36.cloned.1.call-update) | async-done | bytes 589840
  802.5 38.1 %reduce-scatter.26.cloned.1.call-done = bf16[192,1152]{1,0:T(8,128)(2,1)} async-done(((bf16[768,1152]{1,0:T(8,128)(2,1)}), bf16[192,1152]{1,0:T(8,128)(2,1)}) %reduce-scatter.26.cloned.1.call-update) | async-done | bytes 442384
  844.8 19.6 %reduce-scatter.22.cloned.1.call-done = bf16[384,192]{0,1:T(8,128)(2,1)} async-done(((bf16[384,768]{0,1:T(8,128)(2,1)}), bf16[384,192]{0,1:T(8,128)(2,1)}) %reduce-scatter.22.cloned.1.call-update) | async-done | bytes 147472 | tf_op jit(solution)/shard_map/reduce_scatter | solution.py:272
  864.4 48.5 %reduce-scatter.24.cloned.1.call-done = bf16[384,768]{1,0:T(8,128)(2,1)} async-done(((bf16[1536,768]{1,0:T(8,128)(2,1)}), bf16[384,768]{1,0:T(8,128)(2,1)}) %reduce-scatter.24.cloned.1.call-update) | async-done | bytes 589840 | tf_op jit(solution)/shard_map/reduce_scatter | solution.py:290
  914.2 9.9 all-reduce
  924.2 9.3 reduce-scatter.28.cloned.1.call-done
  934.4 18.9 %reduce-scatter.32.cloned.1.call-done = bf16[192,2]{1,0:T(8,128)(2,1)} async-done(((bf16[768,2]{1,0:T(8,128)(2,1)}), bf16[192,2]{1,0:T(8,128)(2,1)}) %reduce-scatter.32.cloned.1.call-update) | async-done | bytes 784
  954.2 19.6 %reduce-scatter.30.cloned.1.call-done = bf16[192,2]{1,0:T(8,128)(2,1)} async-done(((bf16[768,2]{1,0:T(8,128)(2,1)}), bf16[192,2]{1,0:T(8,128)(2,1)}) %reduce-scatter.30.cloned.1.call-update) | async-done | bytes 784
  974.6 19.0 %reduce-scatter.34.cloned.1.call-done = bf16[192,2]{1,0:T(8,128)(2,1)} async-done(((bf16[768,2]{1,0:T(8,128)(2,1)}), bf16[192,2]{1,0:T(8,128)(2,1)}) %reduce-scatter.34.cloned.1.call-update) | async-done | bytes 784
  994.5 10.0 all-reduce.1
  1007.5 7.8 all-reduce.15.cloned.1.call-done
  1015.2 3.0 add_convert_fusion.2
  1018.2 70.0 %all-reduce.17.cloned.1.call-done = (bf16[3,192,384]{1,2,0:T(8,128)(2,1)}, bf16[384,192]{0,1:T(8,128)(2,1)}, bf16[768,384]{1,0:T(8,128)(2,1)}, bf16[384,768]{1,0:T(8,128)(2,1)}) async-done(((bf16[3,192,384]{1,2,0:T(8,128)(2,1)}, bf16[384,192]{0,1:T(8,128)(2,1)}, bf16[768,384]{1,0:T(8,128)(2,1)}, bf16[384,768]{1,0:T(8,128)(2,1)}), (bf16[3,192,384]{1,2,0:T(8,128)(2,1)}, bf16[384,192]{0,1:T(8,128)(2,1)}, ...) | async-done | bytes 1769488 | tf_op jit(solution)/shard_map/psum | solution.py:295
  1088.3 2.2 convert_element_type.284
  (493 shorter events, 191.3 us)
Async XLA Ops:
  7.2 54.9 %all-gather.12.cloned.1.call-start = ((), (), s32[]{:S(2)}) async-start(), calls=%async_computation.9 | async-start | bytes 2211840 | tf_op jit(solution)/shard_map/all_gather | solution.py:131
  7.9 261.8 %all-reduce.9.cloned.1.call-start = ((), (), s32[]{:S(2)}) async-start(), calls=%async_computation.10 | async-start | bytes 6291456 | tf_op jit(solution)/shard_map/psum | solution.py:169
  69.5 10.8 collective-permute-start
  80.4 18.4 %collective-permute-start.1 = (bf16[2,512,384]{1,2,0:T(8,128)(2,1)S(1)}, bf16[2,512,384]{1,2,0:T(8,128)(2,1)S(1)}, u32[]{:S(2)}, u32[]{:S(2)}) collective-permute-start(bf16[2,512,384]{1,2,0:T(8,128)(2,1)S(1)} %pad_maximum_fusion.14), channel_id=1, source_target_pairs={{0,4},{2,6},{4,0},{6,2},{1,5},{3,7},{5,1},{7,3},{8,12},{10,14},{12... | collective-permute-start | bytes 2359304 | tf_op jit(solution)/shard_map/while/body/eval_jaxpr/ppermute | solution.py:39
  111.7 9.8 collective-permute-start
  121.6 16.7 %collective-permute-start.1 = (bf16[2,512,384]{1,2,0:T(8,128)(2,1)S(1)}, bf16[2,512,384]{1,2,0:T(8,128)(2,1)S(1)}, u32[]{:S(2)}, u32[]{:S(2)}) collective-permute-start(bf16[2,512,384]{1,2,0:T(8,128)(2,1)S(1)} %pad_maximum_fusion.14), channel_id=1, source_target_pairs={{0,4},{2,6},{4,0},{6,2},{1,5},{3,7},{5,1},{7,3},{8,12},{10,14},{12... | collective-permute-start | bytes 2359304 | tf_op jit(solution)/shard_map/while/body/eval_jaxpr/ppermute | solution.py:39
  151.2 8.8 collective-permute-start
  160.1 14.9 %collective-permute-start.1 = (bf16[2,512,384]{1,2,0:T(8,128)(2,1)S(1)}, bf16[2,512,384]{1,2,0:T(8,128)(2,1)S(1)}, u32[]{:S(2)}, u32[]{:S(2)}) collective-permute-start(bf16[2,512,384]{1,2,0:T(8,128)(2,1)S(1)} %pad_maximum_fusion.14), channel_id=1, source_target_pairs={{0,4},{2,6},{4,0},{6,2},{1,5},{3,7},{5,1},{7,3},{8,12},{10,14},{12... | collective-permute-start | bytes 2359304 | tf_op jit(solution)/shard_map/while/body/eval_jaxpr/ppermute | solution.py:39
  187.9 10.5 collective-permute-start
  198.5 14.9 %collective-permute-start.1 = (bf16[2,512,384]{1,2,0:T(8,128)(2,1)S(1)}, bf16[2,512,384]{1,2,0:T(8,128)(2,1)S(1)}, u32[]{:S(2)}, u32[]{:S(2)}) collective-permute-start(bf16[2,512,384]{1,2,0:T(8,128)(2,1)S(1)} %pad_maximum_fusion.14), channel_id=1, source_target_pairs={{0,4},{2,6},{4,0},{6,2},{1,5},{3,7},{5,1},{7,3},{8,12},{10,14},{12... | collective-permute-start | bytes 2359304 | tf_op jit(solution)/shard_map/while/body/eval_jaxpr/ppermute | solution.py:39
  224.4 4.3 copy-start.7
  228.7 11.0 copy-start.20
  228.7 18.8 %copy-start.21 = (bf16[2,192]{1,0:T(2,128)(2,1)S(1)}, bf16[2,192]{1,0:T(2,128)(2,1)}, u32[]{:S(2)}) copy-start(bf16[2,192]{1,0:T(2,128)(2,1)} %param.24) | copy-start | bytes 2308
  228.7 28.4 %copy-start.22 = (bf16[384]{0:T(512)(128)(2,1)S(1)}, bf16[384]{0:T(512)(128)(2,1)}, u32[]{:S(2)}) copy-start(bf16[384]{0:T(512)(128)(2,1)} %param.26) | copy-start | bytes 2308
  228.8 79.0 %all-gather.14.cloned.1.call-start = ((), (), s32[]{:S(2)}) async-start(), calls=%async_computation.11 | async-start | bytes 2949120 | tf_op jit(solution)/shard_map/all_gather | solution.py:137
  229.5 129.0 %all-gather.16.cloned.1.call-start = ((), (), s32[]{:S(2)}) async-start(), calls=%async_computation.12 | async-start | bytes 2949120 | tf_op jit(solution)/shard_map/all_gather | solution.py:139
  230.1 157.5 %all-reduce.11.cloned.1.call-start = ((), (), s32[]{:S(2)}) async-start(), calls=%async_computation.13 | async-start | bytes 6291456 | tf_op jit(solution)/shard_map/psum | solution.py:184
  365.4 69.1 %all-reduce.13.cloned.1.call-start = ((), (), s32[]{:S(2)}) async-start(), calls=%async_computation.14 | async-start | bytes 6291456 | tf_op jit(solution)/shard_map/psum | solution.py:211
  387.6 10.9 slice-start.2
  392.0 6.4 slice-start.3
  393.6 4.8 slice-start
  393.6 4.8 slice-start.1
  396.4 2.9 copy-start.25
  398.4 5.5 copy-start.9
  399.3 6.2 copy-start.24
  439.7 2.5 copy-start.3
  440.0 2.1 copy-start.11
  442.4 36.4 %copy-start.12 = (bf16[4,256,384]{2,1,0:T(8,128)(2,1)}, bf16[4,256,384]{2,1,0:T(8,128)(2,1)S(1)}, u32[]{:S(2)}) copy-start(bf16[4,256,384]{2,1,0:T(8,128)(2,1)S(1)} %get-tuple-element.603) | copy-start | bytes 2359300 | tf_op jit(solution)/shard_map/while
  442.4 34.9 %all-gather.18.cloned.1.call-start = ((), (), s32[]{:S(2)}) async-start(), calls=%async_computation.25 | async-start | bytes 1966080 | tf_op jit(solution)/shard_map/while/body/eval_jaxpr/all_gather | solution.py:66
  444.5 73.6 %reduce-scatter.38.cloned.1.call-start = ((), (), s32[]{:S(2)}) async-start(), calls=%async_computation.26 | async-start | bytes 1966080 | tf_op jit(solution)/shard_map/while/body/eval_jaxpr/reduce_scatter | solution.py:110
  478.9 2.7 copy-start
  488.3 31.7 %copy-start.13 = (bf16[4,256,384]{2,1,0:T(8,128)(2,1)S(1)}, bf16[4,256,384]{2,1,0:T(8,128)(2,1)}, u32[]{:S(2)}) copy-start(bf16[4,256,384]{2,1,0:T(8,128)(2,1)} %copy-done.12) | copy-start | bytes 2359300 | tf_op jit(solution)/shard_map/while
  520.0 35.1 %copy-start.12 = (bf16[4,256,384]{2,1,0:T(8,128)(2,1)}, bf16[4,256,384]{2,1,0:T(8,128)(2,1)S(1)}, u32[]{:S(2)}) copy-start(bf16[4,256,384]{2,1,0:T(8,128)(2,1)S(1)} %get-tuple-element.603) | copy-start | bytes 2359300 | tf_op jit(solution)/shard_map/while
  520.0 33.6 %all-gather.18.cloned.1.call-start = ((), (), s32[]{:S(2)}) async-start(), calls=%async_computation.25 | async-start | bytes 1966080 | tf_op jit(solution)/shard_map/while/body/eval_jaxpr/all_gather | solution.py:66
  522.1 72.4 %reduce-scatter.38.cloned.1.call-start = ((), (), s32[]{:S(2)}) async-start(), calls=%async_computation.26 | async-start | bytes 1966080 | tf_op jit(solution)/shard_map/while/body/eval_jaxpr/reduce_scatter | solution.py:110
  555.3 2.7 copy-start
  564.8 31.7 %copy-start.13 = (bf16[4,256,384]{2,1,0:T(8,128)(2,1)S(1)}, bf16[4,256,384]{2,1,0:T(8,128)(2,1)}, u32[]{:S(2)}) copy-start(bf16[4,256,384]{2,1,0:T(8,128)(2,1)} %copy-done.12) | copy-start | bytes 2359300 | tf_op jit(solution)/shard_map/while
  596.5 35.1 %copy-start.12 = (bf16[4,256,384]{2,1,0:T(8,128)(2,1)}, bf16[4,256,384]{2,1,0:T(8,128)(2,1)S(1)}, u32[]{:S(2)}) copy-start(bf16[4,256,384]{2,1,0:T(8,128)(2,1)S(1)} %get-tuple-element.603) | copy-start | bytes 2359300 | tf_op jit(solution)/shard_map/while
  596.5 33.6 %all-gather.18.cloned.1.call-start = ((), (), s32[]{:S(2)}) async-start(), calls=%async_computation.25 | async-start | bytes 1966080 | tf_op jit(solution)/shard_map/while/body/eval_jaxpr/all_gather | solution.py:66
  598.5 72.4 %reduce-scatter.38.cloned.1.call-start = ((), (), s32[]{:S(2)}) async-start(), calls=%async_computation.26 | async-start | bytes 1966080 | tf_op jit(solution)/shard_map/while/body/eval_jaxpr/reduce_scatter | solution.py:110
  631.7 2.7 copy-start
  641.2 31.7 %copy-start.13 = (bf16[4,256,384]{2,1,0:T(8,128)(2,1)S(1)}, bf16[4,256,384]{2,1,0:T(8,128)(2,1)}, u32[]{:S(2)}) copy-start(bf16[4,256,384]{2,1,0:T(8,128)(2,1)} %copy-done.12) | copy-start | bytes 2359300 | tf_op jit(solution)/shard_map/while
  672.9 35.1 %copy-start.12 = (bf16[4,256,384]{2,1,0:T(8,128)(2,1)}, bf16[4,256,384]{2,1,0:T(8,128)(2,1)S(1)}, u32[]{:S(2)}) copy-start(bf16[4,256,384]{2,1,0:T(8,128)(2,1)S(1)} %get-tuple-element.603) | copy-start | bytes 2359300 | tf_op jit(solution)/shard_map/while
  672.9 33.6 %all-gather.18.cloned.1.call-start = ((), (), s32[]{:S(2)}) async-start(), calls=%async_computation.25 | async-start | bytes 1966080 | tf_op jit(solution)/shard_map/while/body/eval_jaxpr/all_gather | solution.py:66
  674.9 72.4 %reduce-scatter.38.cloned.1.call-start = ((), (), s32[]{:S(2)}) async-start(), calls=%async_computation.26 | async-start | bytes 1966080 | tf_op jit(solution)/shard_map/while/body/eval_jaxpr/reduce_scatter | solution.py:110
  708.2 2.7 copy-start
  717.6 31.7 %copy-start.13 = (bf16[4,256,384]{2,1,0:T(8,128)(2,1)S(1)}, bf16[4,256,384]{2,1,0:T(8,128)(2,1)}, u32[]{:S(2)}) copy-start(bf16[4,256,384]{2,1,0:T(8,128)(2,1)} %copy-done.12) | copy-start | bytes 2359300 | tf_op jit(solution)/shard_map/while
  749.4 51.0 %reduce-scatter.36.cloned.1.call-start = ((), (), s32[]{:S(2)}) async-start(), calls=%async_computation.23 | async-start | bytes 2949120
  749.9 90.6 %reduce-scatter.26.cloned.1.call-start = ((), (), s32[]{:S(2)}) async-start(), calls=%async_computation.18 | async-start | bytes 2211840
  761.0 3.8 copy-start.10
  761.0 103.3 %reduce-scatter.22.cloned.1.call-start = ((), (), s32[]{:S(2)}) async-start(), calls=%async_computation.16 | async-start | bytes 737280 | tf_op jit(solution)/shard_map/reduce_scatter | solution.py:272
  764.5 6.4 copy-start.18
  764.5 148.4 %reduce-scatter.24.cloned.1.call-start = ((), (), s32[]{:S(2)}) async-start(), calls=%async_computation.17 | async-start | bytes 2949120 | tf_op jit(solution)/shard_map/reduce_scatter | solution.py:290
  770.8 1.9 copy-start.14
  770.9 162.7 %reduce-scatter.28.cloned.1.call-start = ((), (), s32[]{:S(2)}) async-start(), calls=%async_computation.19 | async-start | bytes 20480
  775.2 178.1 %reduce-scatter.32.cloned.1.call-start = ((), (), s32[]{:S(2)}) async-start(), calls=%async_computation.21 | async-start | bytes 245760
  776.2 197.6 %reduce-scatter.30.cloned.1.call-start = ((), (), s32[]{:S(2)}) async-start(), calls=%async_computation.20 | async-start | bytes 245760
  777.1 216.5 %reduce-scatter.34.cloned.1.call-start = ((), (), s32[]{:S(2)}) async-start(), calls=%async_computation.22 | async-start | bytes 245760
  778.1 237.2 %all-reduce.15.cloned.1.call-start = ((), (), s32[]{:S(2)}) async-start(), calls=%async_computation.15 | async-start | bytes 3145728 | tf_op jit(solution)/shard_map/psum | solution.py:252
  783.5 129.5 %copy-start.26 = (u32[32]{0:T(128)S(1)}, u32[32]{0:T(128)}, u32[]{:S(2)}) copy-start(u32[32]{0:T(128)} %constant.210) | copy-start | bytes 388
  783.5 231.7 %copy-start.4 = (f32[1024,768]{1,0:T(8,128)S(1)}, f32[1024,768]{1,0:T(8,128)}, u32[]{:S(2)}) copy-start(f32[1024,768]{1,0:T(8,128)} %copy-done.3) | copy-start | bytes 9437188
  783.5 304.7 %all-reduce.17.cloned.1.call-start = ((), (), s32[]{:S(2)}) async-start(), calls=%async_computation.24 | async-start | bytes 3833856 | tf_op jit(solution)/shard_map/psum | solution.py:295
  1088.2 4.4 copy-start.16
  1088.3 5.5 copy-start.17
  (12 other events, 17.4 us)
Sparse Core Ops, SparseCore 0:
  9.6 52.4 all-gather.11
  228.9 25.5 all-reduce.8
  256.2 51.4 all-gather.13
  309.2 49.1 all-gather.15
  365.5 22.0 all-reduce.10
  410.0 24.3 all-reduce.12
  445.2 31.9 all-gather.17
  487.1 30.9 reduce-scatter.37
  522.8 30.7 all-gather.17
  563.5 30.9 reduce-scatter.37
  599.3 30.7 all-gather.17
  639.9 30.9 reduce-scatter.37
  675.7 30.7 all-gather.17
  716.4 30.9 reduce-scatter.37
  752.3 47.9 reduce-scatter.35
  802.6 37.8 reduce-scatter.25
  843.2 21.0 reduce-scatter.21
  866.5 46.3 reduce-scatter.23
  915.1 18.3 reduce-scatter.27
  935.8 17.4 reduce-scatter.31
  956.1 17.5 reduce-scatter.29
  976.1 17.4 reduce-scatter.33
  996.6 18.6 all-reduce.14
  1019.6 68.6 all-reduce.16
